TPU v7x, 256 devices: a whole 4x4x8 slice. The times are simulated.
256 devices in a mesh: blk: 32 (over x, z), leaf: 4 (over y), samp: 2 (over core).
Axes of the slice: x: 4, y: 4, z: 8, core: 2. Of those that a mesh axis runs over, the one named last changes fastest.
Arguments:
- points: float32 [3, 32768], P(None, ('blk', 'leaf')), may hold values from 0 to 64, as said below
- neighbors: int32 [128, 8], P(('blk', 'leaf')), may hold values from -1 to 127, as said below
- omega: float32 [512, 32768], P(None, ('blk', 'leaf')), may hold values from -6 to 6
- observed: float32 [32768], P(('blk', 'leaf')), may hold values from -6 to 6
- prior_draws: float32 [64, 32768], P('samp', ('blk', 'leaf')), may hold values from -6 to 6
Outputs:
- weights: float32 [64, 32768], P('samp', ('blk', 'leaf'))
- residual: float32 [64, 32768], P('samp', ('blk', 'leaf'))
Inputs may be any that keep to these rules, and one draw needn't show every extreme that they name: Block g's points lie in the unit cell with integer corner (cx, cy, cz), where cx // 2 = g // 4 and 0 <= cy, cz < 3. `neighbors`: row g lists in ascending order every block h whose unit cell touches g's (cells at most one apart in every coordinate, the first taken periodic of period 2 * 32), which includes every block with a point within distance 1 of a point of g, followed by -1 in the unused slots; the relation is symmetric, and every listed block has a slab index h // 4 equal to or cyclically next to g // 4.
All inputs are finite; a program needn't handle non-finite values.
Results may differ from a plain program's by a relative error of at most 0.0003.
Values sent between devices are 32-bit elements; how exact they have to be, the bound alone decides.
A program may use at most 64 MiB of HBM per device.

v0:
```python
import jax
import jax.numpy as jnp
from jax import lax
from jax.sharding import PartitionSpec as P

PB = 256
ITERS = 2
support_radius = 0.8
noise_variance = 1.0
sketch_shift = 1.0


def shifted_2(block, axis, distance):
    devices = range(lax.axis_size(axis))
    route = [((i - distance) % len(devices), i) for i in devices]
    return lax.ppermute(block, axis, route)


def wendland(row_points, column_points, period):
    offset = row_points[None, :, :, None] - column_points[:, :, None, :]
    half_period = 0.5 * period
    along_x = jnp.mod(offset[:, 0] + half_period, period) - half_period
    squared = along_x * along_x + offset[:, 1] * offset[:, 1] + offset[:, 2] * offset[:, 2]
    radius = jnp.sqrt(squared) / support_radius
    remain = jnp.maximum(1.0 - radius, 0.0)
    return remain**4 * (4.0 * radius + 1.0)


def high_dot(left, right):
    return jnp.dot(left, right, precision=lax.Precision.HIGHEST, preferred_element_type=jnp.float32)


def shifted(values, offset_by):
    return shifted_2(values, "blk", offset_by)


def beside_all(values):
    slab_values = lax.all_gather(values, "leaf", axis=1, tiled=True)
    return jnp.concatenate([shifted(slab_values, 1), slab_values, shifted(slab_values, -1)], axis=1)


def total(values):
    return lax.psum(values, ("blk", "leaf"))


def lower_solve(factor, values):
    return lax.linalg.triangular_solve(factor, values, left_side=True, lower=True)


def local(points, neighbors, omega, observed, prior_draws):
    blk_dev = neighbors.shape[0]
    cycle_count = lax.axis_size("blk")
    slab_blocks = blk_dev * lax.axis_size("leaf")
    period = 2.0 * cycle_count
    own_slab = lax.axis_index("blk")
    usable = neighbors >= 0
    relative = jnp.mod(neighbors // slab_blocks - own_slab + 1, cycle_count)
    chosen = jnp.where(usable, relative * slab_blocks + jnp.mod(neighbors, slab_blocks), 0)
    usable_weight = usable.astype(jnp.float32)
    reach_points = beside_all(points)
    reach_blocks = reach_points.reshape(3, 3 * slab_blocks, PB).transpose(1, 0, 2)
    row_blocks = points.reshape(3, blk_dev, PB).transpose(1, 0, 2)

    def build_tile(block_index):
        kernel_tile = wendland(row_blocks[block_index], reach_blocks[chosen[block_index]], period)
        return kernel_tile * usable_weight[block_index][:, None, None]

    def apply_kernel(values):
        width = values.shape[0]
        reach = beside_all(values).reshape(width, 3 * slab_blocks, PB)
        picked = jnp.take(reach, chosen[0], axis=1)
        pieces = jnp.einsum("cnj,nij->ci", picked, build_tile(0), precision=lax.Precision.HIGHEST)
        return pieces

    sketch = apply_kernel(omega) + sketch_shift * omega
    core_gram = total(high_dot(omega, sketch.T))
    core_gram = 0.5 * (core_gram + core_gram.T)
    factor = jnp.linalg.cholesky(core_gram)
    basis = lower_solve(factor, sketch)
    basis_gram = total(high_dot(basis, basis.T))
    woodbury = noise_variance * jnp.eye(basis.shape[0], dtype=jnp.float32) + 0.5 * (
        basis_gram + basis_gram.T
    )
    wood_factor = jnp.linalg.cholesky(woodbury)

    def inverse_apply(vectors):
        projected = total(high_dot(basis, vectors.T))
        first_solve = lower_solve(wood_factor, projected)
        solved = lax.linalg.triangular_solve(
            wood_factor, first_solve, left_side=True, lower=True, transpose_a=True
        )
        return (vectors - high_dot(solved.T, basis)) / noise_variance

    rhs = observed[None, :] - prior_draws
    weights = jnp.zeros_like(rhs)
    residual = rhs
    precond = inverse_apply(residual)
    direction = precond
    inner_now = total(jnp.sum(residual * precond, axis=1))
    for step_index in range(ITERS):
        image = apply_kernel(direction) + noise_variance * direction
        step_size = inner_now / total(jnp.sum(direction * image, axis=1))
        weights = weights + step_size[:, None] * direction
        residual = residual - step_size[:, None] * image
        if step_index + 1 < ITERS:
            precond = inverse_apply(residual)
            inner_next = total(jnp.sum(residual * precond, axis=1))
            direction = precond + (inner_next / inner_now)[:, None] * direction
            inner_now = inner_next
    return (weights, residual)


def solution(mesh):
    in_specs = (
        P(None, ("blk", "leaf")),
        P(("blk", "leaf"), None),
        P(None, ("blk", "leaf")),
        P(("blk", "leaf")),
        P("samp", ("blk", "leaf")),
    )
    out_specs = (P("samp", ("blk", "leaf")), P("samp", ("blk", "leaf")))
    return jax.shard_map(local, mesh=mesh, in_specs=in_specs, out_specs=out_specs, check_vma=False)
```

profile of v0, /device:TPU:8, one launch (start us, length us, event | category | flops | bytes accessed | tf_op | source)
XLA Modules:
  0.0 2182.1 jit_solution(1720659250722919533)
XLA Ops:
  9.3 12.3 all_gather.13
  29.7 15.5 all-gather.2.cloned.1.call-done
  56.6 39.3 %collective-permute-done.1 = f32[512,1024]{0,1:T(8,128)} collective-permute-done((f32[512,1024]{0,1:T(8,128)}, f32[512,1024]{0,1:T(8,128)}, u32[]{:S(2)}, u32[]{:S(2)}) %collective-permute-start.1) | collective-permute-done | bytes 2097184 | tf_op jit(solution)/shard_map/ppermute | solution.py:16
  127.7 214.8 %all-reduce.7.cloned.1.call-done = f32[512,512]{1,0:T(8,128)} async-done(((f32[512,512]{1,0:T(8,128)}), f32[512,512]{1,0:T(8,128)}) %all-reduce.7.cloned.1.call-update) | async-done | bytes 1048592 | tf_op jit(solution)/shard_map/psum | solution.py:43
  350.6 11.7 cholesky.286
  374.8 11.7 cholesky.305
  386.6 10.2 custom-call.36
  398.3 11.7 cholesky.326
  422.1 11.9 cholesky.343
  439.0 11.7 while.9
  450.7 39.3 %custom-call.29 = f32[4,128,128]{1,2,0:T(8,128)S(1)} custom-call(f32[4,128,128]{2,1,0:T(8,128)S(1)} %get-tuple-element.29), custom_call_target="InvertDiagBlocksLowerTriangular" | custom-call | tf_op jit(solution)/shard_map/triangular_solve | solution.py:47
  499.4 218.7 %all-reduce.11.cloned.1.call-done = (f32[512,512]{1,0:T(8,128)}, f32[512,32]{0,1:T(8,128)}) async-done(((f32[512,512]{1,0:T(8,128)}, f32[512,32]{0,1:T(8,128)}), (f32[512,512]{1,0:T(8,128)}, f32[512,32]{0,1:T(8,128)})) %all-reduce.11.cloned.1.call-update) | async-done | bytes 1114128 | tf_op jit(solution)/shard_map/psum | solution.py:43
  726.3 11.7 cholesky.358
  751.8 11.7 cholesky.377
  764.2 10.2 custom-call.39
  776.8 11.7 cholesky.398
  800.5 11.9 cholesky.415
  826.3 40.1 %custom-call.42 = f32[4,128,128]{1,2,0:T(8,128)S(1)} custom-call(f32[4,128,128]{2,1,0:T(8,128)} %copy-done.13), custom_call_target="InvertDiagBlocksLowerTriangular" | custom-call | tf_op jit(solution)/shard_map/triangular_solve/custom-call.9 | solution.py:89
  873.7 11.9 all_gather.14
  903.9 344.3 %all-reduce.1 = (f32[32]{0:T(128)}, f32[32]{0:T(128)}) all-reduce(f32[32]{0:T(128)} %get-tuple-element.47, f32[32]{0:T(128)S(1)} %get-tuple-element.46), channel_id=1, replica_groups=mesh['blk'=32,'leaf'=4,'samp'=2] {'blk','leaf'}, use_global_device_ids=true, to_apply=%region_12.16 | all-reduce | flops 64 | bytes 512 | tf_op jit(solution)/shard_map/psum | solution.py:43
  1252.6 201.5 %all-reduce.9.cloned.1.call-done = f32[512,32]{0,1:T(8,128)} async-done(((f32[512,32]{0,1:T(8,128)}), f32[512,32]{0,1:T(8,128)}) %all-reduce.9.cloned.1.call-update) | async-done | bytes 65552 | tf_op jit(solution)/shard_map/psum | solution.py:43
  1461.5 342.7 %psum.62 = f32[32]{0:T(128)S(1)} all-reduce(f32[32]{0:T(128)S(1)} %get-tuple-element.101), channel_id=1, replica_groups=mesh['blk'=32,'leaf'=4,'samp'=2] {'blk','leaf'}, use_global_device_ids=true, to_apply=%region_17.22 | all-reduce | flops 32 | bytes 256 | tf_op jit(solution)/shard_map/psum | solution.py:43
  1805.6 12.6 all_gather.15
  1829.6 345.1 %psum.63 = f32[32]{0:T(128)S(1)} all-reduce(f32[32]{0:T(128)S(1)} %get-tuple-element.103), channel_id=1, replica_groups=mesh['blk'=32,'leaf'=4,'samp'=2] {'blk','leaf'}, use_global_device_ids=true, to_apply=%region_19.24 | all-reduce | flops 32 | bytes 256 | tf_op jit(solution)/shard_map/psum | solution.py:43
  (208 shorter events, 218.2 us)
Async XLA Ops:
  7.2 38.0 %all-gather.2.cloned.1.call-start = ((), (), s32[]{:S(2)}) async-start(), calls=%async_computation | async-start | bytes 2621440 | tf_op jit(solution)/shard_map/all_gather | solution.py:38
  9.3 333.2 %all-reduce.7.cloned.1.call-start = ((), (), s32[]{:S(2)}) async-start(), calls=%async_computation.1 | async-start | bytes 2097152 | tf_op jit(solution)/shard_map/psum | solution.py:43
  21.6 30.4 %collective-permute-start.3 = (f32[3,1024]{1,0:T(4,128)S(1)}, f32[3,1024]{1,0:T(4,128)S(1)}, u32[]{:S(2)}, u32[]{:S(2)}) collective-permute-start(f32[3,1024]{1,0:T(4,128)S(1)} %all_gather.13), channel_id=1, source_target_pairs={{8,0},{16,8},{24,16},{32,24},{40,32},{48,40},{56,48},{64,56},{72,6... | collective-permute-start | bytes 36872 | tf_op jit(solution)/shard_map/ppermute | solution.py:16
  29.7 22.3 %collective-permute-start.2 = (f32[3,1024]{1,0:T(4,128)S(1)}, f32[3,1024]{1,0:T(4,128)S(1)}, u32[]{:S(2)}, u32[]{:S(2)}) collective-permute-start(f32[3,1024]{1,0:T(4,128)S(1)} %all_gather.13), channel_id=1, source_target_pairs={{248,0},{0,8},{8,16},{16,24},{24,32},{32,40},{40,48},{48,56},{56,6... | collective-permute-start | bytes 36872 | tf_op jit(solution)/shard_map/ppermute | solution.py:16
  45.2 50.6 %collective-permute-start.1 = (f32[512,1024]{0,1:T(8,128)}, f32[512,1024]{0,1:T(8,128)}, u32[]{:S(2)}, u32[]{:S(2)}) collective-permute-start(f32[512,1024]{0,1:T(8,128)} %all-gather.2.cloned.1.call-done), channel_id=1, source_target_pairs={{8,0},{16,8},{24,16},{32,24},{40,32},{48,40},{56,48},{64,56},{72,6... | collective-permute-start | bytes 6291464 | tf_op jit(solution)/shard_map/ppermute | solution.py:16
  50.6 50.7 %collective-permute-start = (f32[512,1024]{0,1:T(8,128)}, f32[512,1024]{0,1:T(8,128)}, u32[]{:S(2)}, u32[]{:S(2)}) collective-permute-start(f32[512,1024]{0,1:T(8,128)} %all-gather.2.cloned.1.call-done), channel_id=1, source_target_pairs={{248,0},{0,8},{8,16},{16,24},{24,32},{32,40},{40,48},{48,56},{56,6... | collective-permute-start | bytes 6291464 | tf_op jit(solution)/shard_map/ppermute | solution.py:16
  53.9 47.4 %copy-start.7 = (f32[512,1024]{0,1:T(8,128)S(1)}, f32[512,1024]{0,1:T(8,128)}, u32[]{:S(2)}) copy-start(f32[512,1024]{0,1:T(8,128)} %all-gather.2.cloned.1.call-done) | copy-start | bytes 6291460
  113.5 5.6 copy-start.3
  127.4 590.7 %all-reduce.11.cloned.1.call-start = ((), (), s32[]{:S(2)}) async-start(), calls=%async_computation.3 | async-start | bytes 2228224 | tf_op jit(solution)/shard_map/psum | solution.py:43
  439.0 53.8 %copy-start.2 = (f32[512,256]{1,0:T(8,128)S(1)}, f32[512,256]{1,0:T(8,128)}, u32[]{:S(2)}) copy-start(f32[512,256]{1,0:T(8,128)} %copy-done.1) | copy-start | bytes 1572868
  492.4 5.7 copy-start.14
  492.5 5.7 copy-start.17
  492.8 6.6 copy-start.6
  494.4 5.0 copy-start.8
  496.1 222.1 %copy-start.12 = (f32[128,256]{1,0:T(8,128)}, f32[128,256]{1,0:T(8,128)S(1)}, u32[]{:S(2)}) copy-start(f32[128,256]{1,0:T(8,128)S(1)} %fusion.69) | copy-start | bytes 393220
  499.4 954.7 %all-reduce.9.cloned.1.call-start = ((), (), s32[]{:S(2)}) async-start(), calls=%async_computation.2 | async-start | bytes 131072 | tf_op jit(solution)/shard_map/psum | solution.py:43
  812.4 3.3 copy-start
  873.7 17.1 copy-start.10
  885.6 5.2 collective-permute-start.5
  888.3 8.3 collective-permute-start.4
  1818.3 356.4 %copy-start.11 = (f32[32,256]{1,0:T(8,128)S(1)}, f32[32,256]{1,0:T(8,128)}, u32[]{:S(2)}) copy-start(f32[32,256]{1,0:T(8,128)} %copy-done.10) | copy-start | bytes 98308
  1818.3 356.4 %copy-start.16 = (f32[32,256]{1,0:T(8,128)S(1)}, f32[32,256]{1,0:T(8,128)}, u32[]{:S(2)}) copy-start(f32[32,256]{1,0:T(8,128)} %copy-done.15) | copy-start | bytes 98308
  1818.3 5.0 collective-permute-start.7
  1818.6 8.3 collective-permute-start.6
  (6 other events, 4.8 us)
Sparse Core Ops, SparseCore 0:
  9.8 35.3 all-gather.1
  127.5 214.8 all-reduce.6
  499.5 218.5 all-reduce.10
  1252.7 201.3 all-reduce.8
where the time goes:
time: 2190 us; the launch traced here: 2180 us
  blocking collectives  1070 us (49%)
  waiting for transfers between devices  710 us (32%)
  other arithmetic  262 us (12%)
  matrix products  51.5 us (2%)
  local copies, waits for them, and re-layouts  51.3 us (2%)
    psum x3, blocking collectives, total(): return lax.psum(values, ('blk', 'leaf'))  1030 us
    psum x3, waiting for transfers between devices, total(): return lax.psum(values, ('blk', 'leaf'))  635 us
    another operation x15, other arithmetic, local(): wood_factor = jnp.linalg.cholesky(woodbury)  79.7 us
    another operation x14, other arithmetic, local(): factor = jnp.linalg.cholesky(core_gram)  79 us
    ppermute x8, waiting for transfers between devices, shifted_2(): return lax.ppermute(block, axis, route)  59.7 us
  transfers between devices with their start and end apart: 12, of which 10 were waited for; matrix products, arithmetic and copies ran while one was open for 0% of the time, Pallas kernels for 0%

commit v1 on v0

--- a/solution.py
+++ b/solution.py
@@ -2,6 +2,7 @@
 import jax.numpy as jnp
 from jax import lax
 from jax.sharding import PartitionSpec as P
+from jax.lax import psum
 
 PB = 256
 ITERS = 2
@@ -40,7 +41,13 @@
 
 
 def total(values):
-    return lax.psum(values, ("blk", "leaf"))
+
+    def _hold_points(slab_in, a_name, lane_axis="leaf"):
+        for w in (a_name, lane_axis):
+            slab_in = psum(slab_in, w)
+        return slab_in
+
+    return _hold_points(values, "blk")
 
 
 def lower_solve(factor, values):

time: 2190 us -> 1340 us (0.61)
  blocking collectives: 1070 us -> 280 us
  waiting for transfers between devices: 710 us -> 649 us
    psum x3 -> x6, blocking collectives: 1030 us -> 245 us  [_hold_points(): slab_in = psum(slab_in, w)]
    psum x3 -> x6, waiting for transfers between devices: 635 us -> 574 us  [_hold_points(): slab_in = psum(slab_in, w)]
  transfers between devices with their start and end apart: 12 -> 15, of which waited for: 10 -> 13; matrix products, arithmetic and copies ran while one was open for 0% -> 0% of each run, Pallas kernels for 0% -> 0%
where the time goes in v1:
time: 1340 us; the launch traced here: 1330 us
  waiting for transfers between devices  649 us (48%)
  blocking collectives  280 us (21%)
  other arithmetic  262 us (20%)
  matrix products  51.5 us (4%)
  local copies, waits for them, and re-layouts  51.2 us (4%)
  starting transfers between devices  21.5 us (2%)
  between operations  20.1 us (2%)
    psum x6, waiting for transfers between devices, _hold_points(): slab_in = psum(slab_in, w)  574 us
    psum x6, blocking collectives, _hold_points(): slab_in = psum(slab_in, w)  245 us
    another operation x15, other arithmetic, local(): wood_factor = jnp.linalg.cholesky(woodbury)  79.7 us
    another operation x14, other arithmetic, local(): factor = jnp.linalg.cholesky(core_gram)  79 us
    ppermute x8, waiting for transfers between devices, shifted_2(): return lax.ppermute(block, axis, route)  59.4 us
    another operation x2, other arithmetic, inverse_apply(): lax.linalg.triangular_solve(wood_factor, first_solve, left_side=True, low...  41.5 us
    another operation x3, other arithmetic, lower_solve(): lax.linalg.triangular_solve(factor, values, left_side=True, lower=True)  40.4 us
    all_gather x3, blocking collectives, beside_all(): slab_values = lax.all_gather(values, 'leaf', axis=1, tiled=True)  35.1 us
  transfers between devices with their start and end apart: 15, of which 13 were waited for; matrix products, arithmetic and copies ran while one was open for 0% of the time, Pallas kernels for 0%

profile of v1, /device:TPU:8, one launch (start us, length us, event | category | flops | bytes accessed | tf_op | source)
XLA Modules:
  0.0 1334.5 jit_solution(13698916933156464467)
XLA Ops:
  9.3 12.3 all_gather.13
  29.7 15.5 %all-gather.2.cloned.1.call-done = f32[512,1024]{0,1:T(8,128)} async-done(((f32[512,256]{0,1:T(8,128)}), f32[512,1024]{0,1:T(8,128)}) %all-gather.2.cloned.1.call-update) | async-done | bytes 2097168 | tf_op jit(solution)/shard_map/all_gather | solution.py:39
  56.6 39.3 %collective-permute-done.1 = f32[512,1024]{0,1:T(8,128)} collective-permute-done((f32[512,1024]{0,1:T(8,128)}, f32[512,1024]{0,1:T(8,128)}, u32[]{:S(2)}, u32[]{:S(2)}) %collective-permute-start.1) | collective-permute-done | bytes 2097184 | tf_op jit(solution)/shard_map/ppermute | solution.py:17
  127.5 143.4 %all-reduce.12.cloned.1.call-done = f32[512,512]{1,0:T(8,128)} async-done(((f32[512,512]{1,0:T(8,128)}), f32[512,512]{1,0:T(8,128)}) %all-reduce.12.cloned.1.call-update) | async-done | bytes 1048592 | tf_op jit(solution)/shard_map/psum | solution.py:47
  271.2 49.7 %all-reduce.14.cloned.1.call-done = f32[512,512]{1,0:T(8,128)} async-done(((f32[512,512]{1,0:T(8,128)}), f32[512,512]{1,0:T(8,128)}) %all-reduce.14.cloned.1.call-update) | async-done | bytes 1048592 | tf_op jit(solution)/shard_map/psum | solution.py:47
  328.9 11.7 cholesky.286
  353.2 11.7 cholesky.305
  376.7 11.7 cholesky.326
  400.4 11.9 cholesky.343
  417.3 11.7 while.9
  429.0 39.3 %custom-call.29 = f32[4,128,128]{1,2,0:T(8,128)S(1)} custom-call(f32[4,128,128]{2,1,0:T(8,128)S(1)} %get-tuple-element.29), custom_call_target="InvertDiagBlocksLowerTriangular" | custom-call | tf_op jit(solution)/shard_map/triangular_solve | solution.py:54
  477.8 151.8 %all-reduce.20.cloned.1.call-done = (f32[512,512]{1,0:T(8,128)}, f32[512,32]{0,1:T(8,128)}) async-done(((f32[512,512]{1,0:T(8,128)}, f32[512,32]{0,1:T(8,128)}), (f32[512,512]{1,0:T(8,128)}, f32[512,32]{0,1:T(8,128)})) %all-reduce.20.cloned.1.call-update) | async-done | bytes 1114128 | tf_op jit(solution)/shard_map/psum | solution.py:47
  629.6 50.0 %all-reduce.22.cloned.1.call-done = (f32[512,512]{1,0:T(8,128)}, f32[512,32]{0,1:T(8,128)}) async-done(((f32[512,512]{1,0:T(8,128)}, f32[512,32]{0,1:T(8,128)}), (f32[512,512]{1,0:T(8,128)}, f32[512,32]{0,1:T(8,128)})) %all-reduce.22.cloned.1.call-update) | async-done | bytes 1114128 | tf_op jit(solution)/shard_map/psum | solution.py:47
  687.7 11.7 cholesky.358
  713.2 11.7 cholesky.377
  738.3 11.7 cholesky.398
  762.0 11.9 cholesky.415
  787.8 40.1 %custom-call.42 = f32[4,128,128]{1,2,0:T(8,128)S(1)} custom-call(f32[4,128,128]{2,1,0:T(8,128)} %copy-done.13), custom_call_target="InvertDiagBlocksLowerTriangular" | custom-call | tf_op jit(solution)/shard_map/triangular_solve/custom-call.9 | solution.py:96
  835.2 12.0 all_gather.14
  868.1 70.2 %all-reduce.1 = (f32[32]{0:T(128)}, f32[32]{0:T(128)}) all-reduce(f32[32]{0:T(128)} %get-tuple-element.47, f32[32]{0:T(128)S(1)} %get-tuple-element.46), channel_id=1, replica_groups=mesh['blk'=32,'leaf'=4,'samp'=2] {'blk'}, use_global_device_ids=true, to_apply=%region_15.19 | all-reduce | flops 64 | bytes 512 | tf_op jit(solution)/shard_map/psum | solution.py:47
  952.5 133.6 %all-reduce.16.cloned.1.call-done = f32[512,32]{0,1:T(8,128)} async-done(((f32[512,32]{0,1:T(8,128)}), f32[512,32]{0,1:T(8,128)}) %all-reduce.16.cloned.1.call-update) | async-done | bytes 65552 | tf_op jit(solution)/shard_map/psum | solution.py:47
  1086.1 45.4 %all-reduce.18.cloned.1.call-done = f32[512,32]{0,1:T(8,128)} async-done(((f32[512,32]{0,1:T(8,128)}), f32[512,32]{0,1:T(8,128)}) %all-reduce.18.cloned.1.call-update) | async-done | bytes 65552 | tf_op jit(solution)/shard_map/psum | solution.py:47
  1138.9 75.1 %psum.124 = f32[32]{0:T(128)S(1)} all-reduce(f32[32]{0:T(128)S(1)} %get-tuple-element.105), channel_id=1, replica_groups=mesh['blk'=32,'leaf'=4,'samp'=2] {'blk'}, use_global_device_ids=true, to_apply=%region_23.28 | all-reduce | flops 32 | bytes 256 | tf_op jit(solution)/shard_map/psum | solution.py:47
  1246.7 69.6 %psum.126 = f32[32]{0:T(128)S(1)} all-reduce(f32[32]{0:T(128)S(1)} %get-tuple-element.107), channel_id=1, replica_groups=mesh['blk'=32,'leaf'=4,'samp'=2] {'blk'}, use_global_device_ids=true, to_apply=%region_26.31 | all-reduce | flops 32 | bytes 256 | tf_op jit(solution)/shard_map/psum | solution.py:47
  (220 shorter events, 281.5 us)
Async XLA Ops:
  7.2 38.0 %all-gather.2.cloned.1.call-start = ((), (), s32[]{:S(2)}) async-start(), calls=%async_computation | async-start | bytes 2621440 | tf_op jit(solution)/shard_map/all_gather | solution.py:39
  9.3 261.6 %all-reduce.12.cloned.1.call-start = ((), (), s32[]{:S(2)}) async-start(), calls=%async_computation.1 | async-start | bytes 2097152 | tf_op jit(solution)/shard_map/psum | solution.py:47
  21.6 30.4 %collective-permute-start.3 = (f32[3,1024]{1,0:T(4,128)S(1)}, f32[3,1024]{1,0:T(4,128)S(1)}, u32[]{:S(2)}, u32[]{:S(2)}) collective-permute-start(f32[3,1024]{1,0:T(4,128)S(1)} %all_gather.13), channel_id=1, source_target_pairs={{8,0},{16,8},{24,16},{32,24},{40,32},{48,40},{56,48},{64,56},{72,6... | collective-permute-start | bytes 36872 | tf_op jit(solution)/shard_map/ppermute | solution.py:17
  29.7 22.3 %collective-permute-start.2 = (f32[3,1024]{1,0:T(4,128)S(1)}, f32[3,1024]{1,0:T(4,128)S(1)}, u32[]{:S(2)}, u32[]{:S(2)}) collective-permute-start(f32[3,1024]{1,0:T(4,128)S(1)} %all_gather.13), channel_id=1, source_target_pairs={{248,0},{0,8},{8,16},{16,24},{24,32},{32,40},{40,48},{48,56},{56,6... | collective-permute-start | bytes 36872 | tf_op jit(solution)/shard_map/ppermute | solution.py:17
  45.2 50.6 %collective-permute-start.1 = (f32[512,1024]{0,1:T(8,128)}, f32[512,1024]{0,1:T(8,128)}, u32[]{:S(2)}, u32[]{:S(2)}) collective-permute-start(f32[512,1024]{0,1:T(8,128)} %all-gather.2.cloned.1.call-done), channel_id=1, source_target_pairs={{8,0},{16,8},{24,16},{32,24},{40,32},{48,40},{56,48},{64,56},{72,6... | collective-permute-start | bytes 6291464 | tf_op jit(solution)/shard_map/ppermute | solution.py:17
  50.6 50.7 %collective-permute-start = (f32[512,1024]{0,1:T(8,128)}, f32[512,1024]{0,1:T(8,128)}, u32[]{:S(2)}, u32[]{:S(2)}) collective-permute-start(f32[512,1024]{0,1:T(8,128)} %all-gather.2.cloned.1.call-done), channel_id=1, source_target_pairs={{248,0},{0,8},{8,16},{16,24},{24,32},{32,40},{40,48},{48,56},{56,6... | collective-permute-start | bytes 6291464 | tf_op jit(solution)/shard_map/ppermute | solution.py:17
  53.9 47.4 %copy-start.7 = (f32[512,1024]{0,1:T(8,128)S(1)}, f32[512,1024]{0,1:T(8,128)}, u32[]{:S(2)}) copy-start(f32[512,1024]{0,1:T(8,128)} %all-gather.2.cloned.1.call-done) | copy-start | bytes 6291460
  127.4 193.4 %all-reduce.14.cloned.1.call-start = ((), (), s32[]{:S(2)}) async-start(), calls=%async_computation.2 | async-start | bytes 2097152 | tf_op jit(solution)/shard_map/psum | solution.py:47
  270.9 358.6 %all-reduce.20.cloned.1.call-start = ((), (), s32[]{:S(2)}) async-start(), calls=%async_computation.5 | async-start | bytes 2228224 | tf_op jit(solution)/shard_map/psum | solution.py:47
  417.3 53.8 %copy-start.2 = (f32[512,256]{1,0:T(8,128)S(1)}, f32[512,256]{1,0:T(8,128)}, u32[]{:S(2)}) copy-start(f32[512,256]{1,0:T(8,128)} %copy-done.1) | copy-start | bytes 1572868
  470.8 5.7 copy-start.14
  470.8 5.7 copy-start.17
  471.1 6.6 copy-start.6
  474.4 155.2 %copy-start.12 = (f32[128,256]{1,0:T(8,128)}, f32[128,256]{1,0:T(8,128)S(1)}, u32[]{:S(2)}) copy-start(f32[128,256]{1,0:T(8,128)S(1)} %fusion.69) | copy-start | bytes 393220
  477.7 201.9 %all-reduce.22.cloned.1.call-start = ((), (), s32[]{:S(2)}) async-start(), calls=%async_computation.6 | async-start | bytes 2228224 | tf_op jit(solution)/shard_map/psum | solution.py:47
  629.6 456.5 %all-reduce.16.cloned.1.call-start = ((), (), s32[]{:S(2)}) async-start(), calls=%async_computation.3 | async-start | bytes 131072 | tf_op jit(solution)/shard_map/psum | solution.py:47
  835.2 20.0 %copy-start.10 = (f32[32,256]{1,0:T(8,128)}, f32[32,256]{1,0:T(8,128)S(1)}, u32[]{:S(2)}) copy-start(f32[32,256]{1,0:T(8,128)S(1)} %convolution_subtract_fusion.10) | copy-start | bytes 98308
  847.2 8.0 collective-permute-start.5
  852.7 8.3 collective-permute-start.4
  952.4 179.0 %all-reduce.18.cloned.1.call-start = ((), (), s32[]{:S(2)}) async-start(), calls=%async_computation.4 | async-start | bytes 131072 | tf_op jit(solution)/shard_map/psum | solution.py:47
  1235.6 91.2 %copy-start.11 = (f32[32,256]{1,0:T(8,128)S(1)}, f32[32,256]{1,0:T(8,128)}, u32[]{:S(2)}) copy-start(f32[32,256]{1,0:T(8,128)} %copy-done.10) | copy-start | bytes 98308
  1235.6 91.2 %copy-start.16 = (f32[32,256]{1,0:T(8,128)S(1)}, f32[32,256]{1,0:T(8,128)}, u32[]{:S(2)}) copy-start(f32[32,256]{1,0:T(8,128)} %copy-done.15) | copy-start | bytes 98308
  1235.6 5.0 collective-permute-start.7
  1235.6 8.4 collective-permute-start.6
  (9 other events, 18.6 us)
Sparse Core Ops, SparseCore 0:
  9.8 35.3 all-gather.1
  127.5 143.3 all-reduce.11
  273.3 47.5 all-reduce.13
  477.8 151.6 all-reduce.19
  632.0 47.5 all-reduce.21
  952.6 133.4 all-reduce.15
  1088.4 43.0 all-reduce.17
